TPU v7x, 32 devices: a whole 2x2x4 slice. The times are simulated.
32 devices in a mesh: dir: 4 (over x, core), tb: 8 (over z, y).
Axes of the slice: x: 2, y: 2, z: 4, core: 2. Of those that a mesh axis runs over, the one named last changes fastest.
Arguments:
- visibilities: bfloat16 [8192, 128], P('tb'), may hold values from -6 to 6
- uv_coords: bfloat16 [2, 8192], P(None, 'tb'), may hold values from -32 to 32
- comp_lm: float32 [2, 12288], P(None, 'dir'), may hold values from -0.25 to 0.25
- spectra: bfloat16 [2, 12288, 128], P(None, 'dir'), may hold values from -0.1875 to 0.1875
- ridge_weight: float32 [128], replicated, may hold values from 32 to 512
- assignment: int32 [12288], P('dir'), may hold values from 0 to 3071, as said below
- peel_order: int32 [12], P('dir'), may hold values from 0 to 2, as said below
- block_tile: int32 [256, 1], P('tb'), may hold values from 0 to 7; in each aligned block of 32 rows (0 to 31, 32 to 63, ...) at most 8 rows name the same one
Outputs:
- residual: bfloat16 [8192, 128], P('tb')
- subgrids: float32 [8, 2, 1024, 128], P('tb', None, 'dir')
Inputs may be any that keep to these rules, and one draw needn't show every extreme that they name: `assignment`: each owner's 3 * 1024 entries are a permutation of its local component numbers. `peel_order`: each owner's 3 entries are a permutation of its directions. `block_tile`: among the 32 blocks of one index of tb no tile is named more than 8 times; every tile is named by some block of the whole array.
All inputs are finite; a program needn't handle non-finite values.
Results may differ from a plain program's by a relative error of at most 0.0064.
Values may be sent and summed in bfloat16 or wider, within the bound.
A program may use at most 64 MiB of HBM per device.

v0:
```python
import functools
import math

import jax
import jax.numpy as jnp
from jax import lax
from jax.experimental import pallas as pl
from jax.experimental.pallas import tpu as pltpu
from jax.sharding import PartitionSpec as P

NCOMP = 1024
GRID = 32
DIR_DEV = 3
ITERS = 4
BB = 32
GB = 128
ROWS_DEV = 1024
PIX = 1024

MESH = pl.DeviceIdType.MESH
F32 = jnp.float32
BF16 = jnp.bfloat16
LANES = 128
CHUNK = 512
SUB = 32

SIN_FIT = (
    4.442882919124344,
    -7.308245686509099,
    3.6063542184331383,
    -0.8461116503741475,
    0.10982451642439378,
)
COS_FIT = (
    1.4142134962552289,
    -6.978850948563853,
    5.7394603769076955,
    -1.8835579059892091,
    0.31068802753070307,
)


def horner(square, fit):
    total = fit[-1]
    for coefficient in fit[-2::-1]:
        total = total * square + coefficient
    return total


def turn_cos_sin(turns):
    part = turns - jnp.round(turns)
    square = part * part
    half_sin = part * horner(square, SIN_FIT)
    half_cos = horner(square, COS_FIT)
    return (1.0 - half_sin * half_sin).astype(BF16), (half_sin * half_cos).astype(BF16)


def kernel(
    owners,
    peers,
    slots,
    vis_ref,
    coord_ref,
    lm_ref,
    spec_ref,
    ridge_ref,
    entry_ref,
    block_of_ref,
    sendc_ref,
    resid_ref,
    grid_ref,
    masked,
    turned_a,
    turned_b,
    acc,
    models_out,
    models_in,
    resid,
    rows_out,
    rows_in,
    coords_in,
    tables,
    m_send,
    m_recv,
    r_send,
    r_recv,
    d_send,
    d_recv,
    c_send,
    c_recv,
):
    me_d = lax.axis_index("dir")
    me_t = lax.axis_index("tb")
    sample_rows, columns = vis_ref.shape
    comps = lm_ref.shape[1]
    group_rows = sample_rows // owners
    block_count = sample_rows // BB
    group_blocks = block_count // owners
    slot_rows = slots * BB

    barrier = pltpu.get_barrier_semaphore()
    for k in range(1, owners):
        pl.semaphore_signal(
            barrier, inc=1, device_id={"dir": lax.rem(me_d + k, owners)}, device_id_type=MESH
        )

    def greet(k, carry):
        pl.semaphore_signal(
            barrier, inc=1, device_id={"tb": lax.rem(me_t + k, peers)}, device_id_type=MESH
        )
        return carry

    lax.fori_loop(1, peers, greet, 0)
    pl.semaphore_wait(barrier, owners - 1 + peers - 1)

    def coords_copy(src, dst, sem, to):
        return pltpu.make_async_remote_copy(
            src_ref=sendc_ref.at[src],
            dst_ref=coords_in.at[dst],
            send_sem=c_send.at[src],
            recv_sem=c_recv.at[sem],
            device_id={"tb": to},
            device_id_type=MESH,
        )

    def send_coords(k, carry):
        to = lax.rem(me_t + k, peers)
        coords_copy(to, me_t, me_t, to).start()
        return carry

    lax.fori_loop(1, peers, send_coords, 0)
    coords_in[pl.ds(me_t, 1)] = sendc_ref[pl.ds(me_t, 1)]

    strips = comps // LANES
    padded = -(-strips // 16) * 16
    named = entry_ref[0:1, :]
    place = entry_ref[1:2, :].astype(F32)
    low = lax.broadcasted_iota(jnp.int32, (LANES, comps), 0)
    high = lax.broadcasted_iota(jnp.int32, (padded, comps), 0)
    at_low = jnp.where(low == named % LANES, 1.0, 0.0).astype(BF16)
    at_high = jnp.where(high == named // LANES, place, 0.0).astype(BF16)
    positions = lax.dot_general(
        at_low, at_high, (((1,), (1,)), ((), ())), preferred_element_type=F32
    )
    for strip in range(strips):
        own = jnp.broadcast_to(positions[:, strip : strip + 1], (LANES, columns))
        span = pl.ds(strip * LANES, LANES)
        for part in range(2):
            values = spec_ref[part, span, :].astype(F32)
            for position in range(DIR_DEV):
                masked[part, span, position * columns : (position + 1) * columns] = jnp.where(
                    own == float(position), values, 0.0
                ).astype(BF16)

    def models_copy(group, owner, to):
        return pltpu.make_async_remote_copy(
            src_ref=models_out.at[group],
            dst_ref=models_in.at[owner],
            send_sem=m_send.at[group],
            recv_sem=m_recv.at[owner],
            device_id={"dir": to},
            device_id_type=MESH,
        )

    def predict_group(k, carry):
        group = lax.rem(me_d + k, owners)
        first = group * group_rows
        for chunk in range(comps // CHUNK):
            turned = turned_a if chunk % 2 == 0 else turned_b
            span = slice(chunk * CHUNK, (chunk + 1) * CHUNK)
            l_row = lm_ref[0:1, span]
            m_row = lm_ref[1:2, span]
            for sub in range(group_rows // SUB):
                coord = coord_ref[pl.ds(pl.multiple_of(first + sub * SUB, SUB), SUB), :]
                cos_part, sin_part = turn_cos_sin(coord[:, 0:1] * l_row + coord[:, 1:2] * m_row)
                turned[0, sub * SUB : (sub + 1) * SUB, :] = cos_part
                turned[1, sub * SUB : (sub + 1) * SUB, :] = sin_part
            update = jnp.dot(turned[0], masked[0, span, :], preferred_element_type=F32) + jnp.dot(
                turned[1], masked[1, span, :], preferred_element_type=F32
            )
            if chunk == 0:
                acc[...] = update
            elif chunk < comps // CHUNK - 1:
                acc[...] += update
            else:
                final = (acc[...] + update).astype(BF16)

        @pl.when(k < owners)
        def _():
            models_out[group] = final
            models_copy(group, me_d, group).start()

        @pl.when(k == owners)
        def _():
            models_in[me_d] = final

        return carry

    lax.fori_loop(1, owners + 1, predict_group, 0)

    def wait_coords(k, carry):
        source = lax.rem(me_t + k, peers)
        coords_copy(source, source, source, source).wait()
        return carry

    lax.fori_loop(1, peers, wait_coords, 0)
    share = grid_ref.shape[1]
    pixel = me_d * share + lax.broadcasted_iota(jnp.int32, (share, 16), 0)
    which = lax.broadcasted_iota(jnp.int32, (share, 16), 1)
    pixel_xy = jnp.where(
        which == 0,
        (pixel // GRID - GRID // 2).astype(F32),
        jnp.where(which == 1, (pixel % GRID - GRID // 2).astype(F32), 0.0),
    )
    pixel_xy = (pixel_xy / (2.0 * GRID)).astype(BF16)

    def make_table(source, carry):
        turns = jnp.dot(pixel_xy, coords_in[source], preferred_element_type=F32)
        cos_part, sin_part = turn_cos_sin(turns)
        tables[source, 0:share, :] = cos_part
        tables[source, share : 2 * share, :] = sin_part
        return carry

    lax.fori_loop(0, peers, make_table, 0)

    def wait_models(k, carry):
        source = lax.rem(me_d + k, owners)
        models_copy(source, source, source).wait()
        return carry

    lax.fori_loop(1, owners, wait_models, 0)

    gain_blocks = group_rows // GB
    first = me_d * group_rows
    ridge = jnp.broadcast_to(ridge_ref[...], (8, columns))
    lane = lax.broadcasted_iota(jnp.int32, (8, columns), 1)

    def over_rows(value):
        total = jnp.sum(jnp.sum(value, axis=0), axis=0, keepdims=True)
        return jnp.broadcast_to(total, (8, columns))

    def peel_owner(owner, remains):
        out = []
        for block in range(gain_blocks):
            rest = remains[block]
            for position in range(DIR_DEV):
                model = models_in[
                    owner,
                    block * GB : (block + 1) * GB,
                    position * columns : (position + 1) * columns,
                ].astype(F32)
                model = model.reshape(GB // 8, 8, columns)
                cross_sum = over_rows(rest * model)
                inverse = 1.0 / (over_rows(model * model) + ridge)
                gain = jnp.ones_like(cross_sum)
                for sweep in range(ITERS):
                    before = jnp.where(lane < 2, gain, pltpu.roll(gain, 2, 1))
                    after = jnp.where(
                        lane >= columns - 2, gain, pltpu.roll(gain, columns - 2, 1)
                    )
                    gain = (cross_sum + ridge * (0.5 * (before + after))) * inverse
                rest = rest - gain[None] * model
            out.append(rest.astype(BF16).astype(F32))
        return tuple(out)

    start = tuple(
        vis_ref[pl.ds(pl.multiple_of(first + block * GB, GB), GB), :]
        .astype(F32)
        .reshape(GB // 8, 8, columns)
        for block in range(gain_blocks)
    )
    done = lax.fori_loop(0, owners, peel_owner, start)
    per_gain = GB // BB
    for block in range(gain_blocks):
        resid[pl.ds(me_d * group_blocks + block * per_gain, per_gain)] = (
            done[block].reshape(per_gain, BB, columns).astype(BF16)
        )
    resid[block_count] = jnp.zeros((BB, columns), BF16)

    def resid_copy(group, sem, to):
        part = pl.ds(group * group_blocks, group_blocks)
        return pltpu.make_async_remote_copy(
            src_ref=resid.at[part],
            dst_ref=resid.at[part],
            send_sem=r_send.at[sem],
            recv_sem=r_recv.at[group],
            device_id={"dir": to},
            device_id_type=MESH,
        )

    for k in range(1, owners):
        to = lax.rem(me_d + k, owners)
        resid_copy(me_d, to, to).start()
    for k in range(1, owners):
        source = lax.rem(me_d + k, owners)
        resid_copy(source, source, source).wait_recv()

    def rows_copy(src, owner, to):
        return pltpu.make_async_remote_copy(
            src_ref=rows_out.at[src],
            dst_ref=rows_in.at[owner],
            send_sem=d_send.at[src],
            recv_sem=d_recv.at[owner],
            device_id={"tb": to},
            device_id_type=MESH,
        )

    def dispatch(k, carry):
        to = lax.rem(me_t + k, peers)
        for slot in range(slots):
            rows_out[to, slot * BB : (slot + 1) * BB, :] = resid[block_of_ref[to * slots + slot]]

        @pl.when(k < peers)
        def _():
            rows_copy(to, me_t, to).start()

        return carry

    lax.fori_loop(1, peers + 1, dispatch, 0)
    resid_ref[...] = resid[0:block_count].reshape(sample_rows, columns)

    grid_sum = jnp.dot(tables[me_t], rows_out[me_t], preferred_element_type=F32)

    def add_source(k, total):
        source = lax.rem(me_t + k, peers)
        rows_copy(source, source, source).wait_recv()
        return total + jnp.dot(tables[source], rows_in[source], preferred_element_type=F32)

    grid_sum = lax.fori_loop(1, peers, add_source, grid_sum)
    grid_ref[...] = (grid_sum * float(ROWS_DEV) ** (-0.5)).reshape(2, share, columns)

    for k in range(1, owners):
        to = lax.rem(me_d + k, owners)
        resid_copy(me_d, to, to).wait_send()

    def drain(k, carry):
        to = lax.rem(me_t + k, peers)
        rows_copy(to, me_t, to).wait_send()
        return carry

    lax.fori_loop(1, peers, drain, 0)


def local(
    owners,
    peers,
    visibilities,
    uv_coords,
    comp_lm,
    spectra,
    ridge_weight,
    assignment,
    peel_order,
    block_tile,
):
    sample_rows, columns = visibilities.shape
    comps = comp_lm.shape[1]
    block_count = sample_rows // BB
    group_rows = sample_rows // owners
    slots = max(2, 2 * block_count // peers)
    share = PIX // owners

    directions = jnp.arange(DIR_DEV, dtype=jnp.int32)
    place = jnp.sum(
        jnp.where(peel_order[:, None] == directions[None, :], directions[:, None], 0), axis=0
    )
    place = jnp.broadcast_to(place[:, None], (DIR_DEV, comps // DIR_DEV)).reshape(comps)
    entries = jnp.stack([assignment, place])

    tile_ids = block_tile[:, 0]
    block_ids = jnp.arange(block_count, dtype=jnp.int32)
    same_tile = tile_ids[:, None] == tile_ids[None, :]
    before = block_ids[None, :] < block_ids[:, None]
    slot_index = jnp.sum(same_tile & before, axis=1, dtype=jnp.int32)
    target = tile_ids * slots + slot_index
    placed = target[None, :] == jnp.arange(peers * slots, dtype=jnp.int32)[:, None]
    block_of = jnp.min(jnp.where(placed, block_ids[None, :], block_count), axis=1)
    block_coords = uv_coords.reshape(2, block_count, BB).transpose(1, 0, 2).reshape(block_count, -1)
    send_coords = jnp.dot(placed.astype(BF16), block_coords, preferred_element_type=F32)
    send_coords = send_coords.astype(BF16).reshape(peers, slots, 2, BB).transpose(0, 2, 1, 3)
    send_coords = jnp.pad(
        send_coords.reshape(peers, 2, slots * BB), ((0, 0), (0, 14), (0, 0))
    )

    vmem = pl.BlockSpec(memory_space=pltpu.VMEM)
    smem = pl.BlockSpec(memory_space=pltpu.SMEM)
    dma = pltpu.SemaphoreType.DMA
    residual, subgrid = pl.pallas_call(
        functools.partial(kernel, owners, peers, slots),
        out_shape=(
            jax.ShapeDtypeStruct((sample_rows, columns), BF16),
            jax.ShapeDtypeStruct((2, share, columns), F32),
        ),
        in_specs=[vmem] * 6 + [smem, vmem],
        out_specs=(vmem, vmem),
        scratch_shapes=[
            pltpu.VMEM((2, comps, DIR_DEV * columns), BF16),
            pltpu.VMEM((2, group_rows, CHUNK), BF16),
            pltpu.VMEM((2, group_rows, CHUNK), BF16),
            pltpu.VMEM((group_rows, DIR_DEV * columns), F32),
            pltpu.VMEM((owners, group_rows, DIR_DEV * columns), BF16),
            pltpu.VMEM((owners, group_rows, DIR_DEV * columns), BF16),
            pltpu.VMEM((block_count + 1, BB, columns), BF16),
            pltpu.VMEM((peers, slots * BB, columns), BF16),
            pltpu.VMEM((peers, slots * BB, columns), BF16),
            pltpu.VMEM((peers, 16, slots * BB), BF16),
            pltpu.VMEM((peers, 2 * share, slots * BB), BF16),
            dma((owners,)),
            dma((owners,)),
            dma((owners,)),
            dma((owners,)),
            dma((peers,)),
            dma((peers,)),
            dma((peers,)),
            dma((peers,)),
        ],
        compiler_params=pltpu.CompilerParams(
            collective_id=0, has_side_effects=True, vmem_limit_bytes=60 * 1024 * 1024
        ),
    )(
        visibilities,
        uv_coords.astype(F32).T,
        comp_lm,
        spectra,
        ridge_weight[None, :],
        entries,
        block_of,
        send_coords,
    )
    return residual, subgrid[None]


def solution(mesh):
    return jax.shard_map(
        functools.partial(local, mesh.shape["dir"], mesh.shape["tb"]),
        mesh=mesh,
        in_specs=(
            P("tb", None),
            P(None, "tb"),
            P(None, "dir"),
            P(None, "dir", None),
            P(),
            P("dir"),
            P("dir"),
            P("tb", None),
        ),
        out_specs=(P("tb", None), P("tb", None, "dir", None)),
        check_vma=False,
    )
```

profile of v0, /device:TPU:13, one launch (start us, length us, event | category | flops | bytes accessed | tf_op | source)
XLA Modules:
  0.0 59.0 jit_solution(13403721361920422647)
XLA Ops:
  0.6 0.7 %select_reduce_fusion.1 = s32[3]{0:T(128)S(1)} fusion(s32[3]{0:T(128)} %param.14), kind=kLoop, calls=%fused_computation.11 | loop fusion | flops 24 | bytes 24 | tf_op jit(solution)/shard_map/reduce_sum | solution.py:364
  1.4 0.9 %convert_reduce_fusion = s32[32]{0:T(128)S(1)} fusion(s32[32]{0:T(128)} %bitcast.26), kind=kLoop, calls=%fused_computation.6 | loop fusion | flops 5088 | bytes 256 | tf_op jit(solution)/shard_map/reduce_sum | solution.py:374
  2.3 0.7 %multiply_add_fusion = s32[32]{0:T(128)S(1)} fusion(s32[32]{0:T(128)S(1)} %convert_reduce_fusion, s32[32,1]{0,1:T(1,128)} %param.15), kind=kLoop, calls=%fused_computation.13 | loop fusion | flops 64 | bytes 384 | tf_op jit(solution)/shard_map/add | solution.py:375
  2.9 0.7 %select_reduce_fusion.block_of_ref = s32[64]{0:T(128)} fusion(s32[32]{0:T(128)S(1)} %multiply_add_fusion), kind=kLoop, calls=%fused_computation.4 | loop fusion | flops 6080 | bytes 384 | tf_op jit(solution)/shard_map/reduce_min | solution.py:377
  3.6 0.1 broadcast_bitcast_fusion
  3.7 1.3 %pad_add_fusion.entry_ref = s32[2,3072]{1,0:T(2,128)} fusion(s32[1,3072]{1,0:T(1,128)S(1)} %bitcast.23, s32[1,3072]{1,0:T(1,128)} %bitcast.24), kind=kLoop, calls=%fused_computation.2 | loop fusion | flops 6144 | bytes 49152 | tf_op jit(solution)/shard_map/stack | solution.py:368
  5.1 0.8 %reshape.27 = bf16[2,32,32]{2,1,0:T(8,128)(2,1)S(1)} reshape(bf16[2,1024]{1,0:T(2,128)(2,1)} %param.9) | data formatting | bytes 8192 | tf_op jit(solution)/shard_map/reshape | solution.py:378
  5.8 0.1 reshape.28
  5.9 0.3 convolution_convert_fusion
  6.2 0.1 reshape.29
  6.3 0.1 reshape.30
  6.4 0.6 %pad.4.sendc_ref = bf16[8,16,256]{2,1,0:T(8,128)(2,1)} pad(bf16[8,2,256]{2,1,0:T(2,128)(2,1)S(1)} %reshape.30, bf16[]{:T(256)} %constant.9.clone.1), padding=0_0x0_14x0_0 | pad | bytes 73730 | tf_op jit(solution)/shard_map/jit(_pad)/pad | solution.py:381
  7.0 1.7 %copy.15 = f32[2,1024]{0,1:T(8,128)} copy(bf16[2,1024]{1,0:T(2,128)(2,1)} %param.9) | data formatting | bytes 12288 | tf_op jit(solution)/shard_map/transpose | solution.py:422
  8.7 46.9 %shard_map.95 = (bf16[1024,128]{1,0:T(8,128)(2,1)}, f32[2,256,128]{2,1,0:T(8,128)}) custom-call(bf16[1024,128]{1,0:T(8,128)(2,1)} %vis_ref.1, f32[1024,2]{1,0:T(8,128)} %bitcast.19, f32[2,3072]{1,0:T(2,128)} %lm_ref.1, bf16[2,3072,128]{2,1,0:T(8,128)(2,1)} %spec_ref.1, f32[1,128]{1,0:T(1,128)} %bitcast.25, s32[2,3072]{1,0:T(2,128)} %pad_add_fusion.entry_ref, ...), custom_call_target="tpu_custom_call" | custom-call | tf_op jit(solution)/shard_map/pallas_call | solution.py:388
  55.6 1.7 %copy.25 = bf16[1024,128]{1,0:T(8,128)(2,1)} copy(bf16[1024,128]{1,0:T(8,128)(2,1)} %get-tuple-element.8) | data formatting | bytes 524288
  57.3 1.7 %copy.26 = f32[1,2,256,128]{3,2,1,0:T(8,128)} copy(f32[1,2,256,128]{3,2,1,0:T(8,128)} %bitcast.20) | data formatting | bytes 524288
  (3 shorter events, 0.0 us)
where the time goes:
time: 59.3 us; the launch traced here: 59 us
  Pallas kernels  46.9 us (79%)
  local copies, waits for them, and re-layouts  6.78 us (11%)
  other arithmetic  4.33 us (7%)
  between operations  0.66 us (1%)
    pallas_call x1, Pallas kernels, local(): pl.pallas_call(functools.partial(kernel, owners, peers, slots), out_shape...  46.9 us
    unnamed x4, local copies, waits for them, and re-layouts  3.42 us
    transpose x1, local copies, waits for them, and re-layouts, local(): uv_coords.astype(F32)  1.65 us
    another operation x1, other arithmetic, local(): entries = jnp.stack([assignment, place])  1.34 us

commit v1 on v0

--- a/solution.py
+++ b/solution.py
@@ -24,20 +24,8 @@
 CHUNK = 512
 SUB = 32
 
-SIN_FIT = (
-    4.442882919124344,
-    -7.308245686509099,
-    3.6063542184331383,
-    -0.8461116503741475,
-    0.10982451642439378,
-)
-COS_FIT = (
-    1.4142134962552289,
-    -6.978850948563853,
-    5.7394603769076955,
-    -1.8835579059892091,
-    0.31068802753070307,
-)
+SIN_FIT = (4.4428795675460835, -7.307816684491791, 3.5977741780872416, -0.7911993921613704)
+COS_FIT = (1.414204014809076, -6.977637323456295, 5.715187874756718, -1.728213892223522)
 
 
 def horner(square, fit):
@@ -60,16 +48,21 @@
     peers,
     slots,
     vis_ref,
-    coord_ref,
+    uv_ref,
     lm_ref,
     spec_ref,
     ridge_ref,
     entry_ref,
-    block_of_ref,
-    sendc_ref,
+    tile_ref,
+    peel_ref,
     resid_ref,
     grid_ref,
     masked,
+    lm_parts,
+    coord_rows,
+    block_row,
+    block_of_ref,
+    coords_out,
     turned_a,
     turned_b,
     acc,
@@ -88,6 +81,7 @@
     d_recv,
     c_send,
     c_recv,
+    index_sem,
 ):
     me_d = lax.axis_index("dir")
     me_t = lax.axis_index("tb")
@@ -113,28 +107,53 @@
     lax.fori_loop(1, peers, greet, 0)
     pl.semaphore_wait(barrier, owners - 1 + peers - 1)
 
-    def coords_copy(src, dst, sem, to):
-        return pltpu.make_async_remote_copy(
-            src_ref=sendc_ref.at[src],
-            dst_ref=coords_in.at[dst],
-            send_sem=c_send.at[src],
-            recv_sem=c_recv.at[sem],
-            device_id={"tb": to},
-            device_id_type=MESH,
-        )
-
-    def send_coords(k, carry):
-        to = lax.rem(me_t + k, peers)
-        coords_copy(to, me_t, me_t, to).start()
-        return carry
-
-    lax.fori_loop(1, peers, send_coords, 0)
-    coords_in[pl.ds(me_t, 1)] = sendc_ref[pl.ds(me_t, 1)]
+    slot_lanes = block_row.shape[1]
+    lane = lax.broadcasted_iota(jnp.int32, (block_count, slot_lanes), 1)
+    tile = jnp.broadcast_to(tile_ref[...], (block_count, slot_lanes))
+    named_tile = jnp.where(lane == tile, 1.0, 0.0)
+    row_id = lax.broadcasted_iota(jnp.int32, (block_count, block_count), 0)
+    earlier = jnp.where(
+        lax.broadcasted_iota(jnp.int32, (block_count, block_count), 1) < row_id, 1.0, 0.0
+    )
+    ranks = jnp.dot(earlier.astype(BF16), named_tile.astype(BF16), preferred_element_type=F32)
+    slot = jnp.sum(ranks * named_tile, axis=1, keepdims=True).astype(jnp.int32)
+    target = tile_ref[...] * slots + slot
+    block_id = lax.broadcasted_iota(jnp.int32, (block_count, slot_lanes), 0)
+    taken = jnp.where(lane == target, block_id, block_count).astype(F32)
+    block_row[...] = jnp.min(taken, axis=0, keepdims=True).astype(jnp.int32)
+    index_copy = pltpu.make_async_copy(block_row, block_of_ref, index_sem)
+    index_copy.start()
+
+    u_row = uv_ref[0:1, :].astype(F32)
+    v_row = uv_ref[1:2, :].astype(F32)
+    stacked = jnp.concatenate(
+        [u_row] * 3 + [v_row] * 3 + [jnp.zeros((LANES - 6, sample_rows), F32)], axis=0
+    )
+    coord_rows[0:block_count] = (
+        stacked.T.astype(BF16).reshape(block_count, BB, LANES)
+    )
+    coord_rows[block_count] = jnp.zeros((BB, LANES), BF16)
+
+    parts = []
+    for which in range(2):
+        left = lm_ref[which : which + 1, :]
+        for part in range(3):
+            rounded = left.astype(BF16).astype(F32)
+            parts.append(rounded)
+            left = left - rounded
+    parts.append(jnp.zeros((2, comps), F32))
+    lm_parts[...] = jnp.concatenate(parts, axis=0).astype(BF16)
 
     strips = comps // LANES
     padded = -(-strips // 16) * 16
-    named = entry_ref[0:1, :]
-    place = entry_ref[1:2, :].astype(F32)
+    named = jnp.concatenate([entry_ref[r : r + 1, :] for r in range(strips)], axis=1)
+    places = []
+    for direction in range(DIR_DEV):
+        value = jnp.int32(0)
+        for position in range(DIR_DEV):
+            value = value + jnp.where(peel_ref[position] == direction, position, 0)
+        places.append(jnp.full((1, comps // DIR_DEV), value, jnp.int32))
+    place = jnp.concatenate(places, axis=1).astype(F32)
     low = lax.broadcasted_iota(jnp.int32, (LANES, comps), 0)
     high = lax.broadcasted_iota(jnp.int32, (padded, comps), 0)
     at_low = jnp.where(low == named % LANES, 1.0, 0.0).astype(BF16)
@@ -152,6 +171,36 @@
                     own == float(position), values, 0.0
                 ).astype(BF16)
 
+    def coords_copy(src, owner, to):
+        return pltpu.make_async_remote_copy(
+            src_ref=coords_out.at[src],
+            dst_ref=coords_in.at[owner],
+            send_sem=c_send.at[src],
+            recv_sem=c_recv.at[owner],
+            device_id={"tb": to},
+            device_id_type=MESH,
+        )
+
+    index_copy.wait()
+
+    def block_in(to, slot):
+        block = block_of_ref[0, to * slots + slot]
+        return jnp.minimum(jnp.maximum(block, 0), block_count)
+
+    def send_coords(k, carry):
+        to = lax.rem(me_t + k, peers)
+        for slot in range(slots):
+            coords_out[to, slot * BB : (slot + 1) * BB, :] = coord_rows[block_in(to, slot)]
+
+        @pl.when(k < peers)
+        def _():
+            coords_copy(to, me_t, to).start()
+
+        return carry
+
+    lax.fori_loop(1, peers + 1, send_coords, 0)
+    coords_in[me_t] = coords_out[me_t]
+
     def models_copy(group, owner, to):
         return pltpu.make_async_remote_copy(
             src_ref=models_out.at[group],
@@ -164,17 +213,17 @@
 
     def predict_group(k, carry):
         group = lax.rem(me_d + k, owners)
-        first = group * group_rows
+        group_coords = coord_rows[pl.ds(group * group_blocks, group_blocks)]
+        group_coords = group_coords.reshape(group_rows, LANES)[:, 0:8]
         for chunk in range(comps // CHUNK):
             turned = turned_a if chunk % 2 == 0 else turned_b
             span = slice(chunk * CHUNK, (chunk + 1) * CHUNK)
-            l_row = lm_ref[0:1, span]
-            m_row = lm_ref[1:2, span]
+            turns = jnp.dot(group_coords, lm_parts[:, span], preferred_element_type=F32)
             for sub in range(group_rows // SUB):
-                coord = coord_ref[pl.ds(pl.multiple_of(first + sub * SUB, SUB), SUB), :]
-                cos_part, sin_part = turn_cos_sin(coord[:, 0:1] * l_row + coord[:, 1:2] * m_row)
-                turned[0, sub * SUB : (sub + 1) * SUB, :] = cos_part
-                turned[1, sub * SUB : (sub + 1) * SUB, :] = sin_part
+                rows = slice(sub * SUB, (sub + 1) * SUB)
+                cos_part, sin_part = turn_cos_sin(turns[rows])
+                turned[0, rows, :] = cos_part
+                turned[1, rows, :] = sin_part
             update = jnp.dot(turned[0], masked[0, span, :], preferred_element_type=F32) + jnp.dot(
                 turned[1], masked[1, span, :], preferred_element_type=F32
             )
@@ -200,22 +249,24 @@
 
     def wait_coords(k, carry):
         source = lax.rem(me_t + k, peers)
-        coords_copy(source, source, source, source).wait()
+        coords_copy(source, source, source).wait()
         return carry
 
     lax.fori_loop(1, peers, wait_coords, 0)
     share = grid_ref.shape[1]
-    pixel = me_d * share + lax.broadcasted_iota(jnp.int32, (share, 16), 0)
-    which = lax.broadcasted_iota(jnp.int32, (share, 16), 1)
+    pixel = me_d * share + lax.broadcasted_iota(jnp.int32, (share, LANES), 0)
+    which = lax.broadcasted_iota(jnp.int32, (share, LANES), 1)
     pixel_xy = jnp.where(
         which == 0,
         (pixel // GRID - GRID // 2).astype(F32),
-        jnp.where(which == 1, (pixel % GRID - GRID // 2).astype(F32), 0.0),
+        jnp.where(which == 3, (pixel % GRID - GRID // 2).astype(F32), 0.0),
     )
     pixel_xy = (pixel_xy / (2.0 * GRID)).astype(BF16)
 
     def make_table(source, carry):
-        turns = jnp.dot(pixel_xy, coords_in[source], preferred_element_type=F32)
+        turns = lax.dot_general(
+            pixel_xy, coords_in[source], (((1,), (1,)), ((), ())), preferred_element_type=F32
+        )
         cos_part, sin_part = turn_cos_sin(turns)
         tables[source, 0:share, :] = cos_part
         tables[source, share : 2 * share, :] = sin_part
@@ -308,7 +359,7 @@
     def dispatch(k, carry):
         to = lax.rem(me_t + k, peers)
         for slot in range(slots):
-            rows_out[to, slot * BB : (slot + 1) * BB, :] = resid[block_of_ref[to * slots + slot]]
+            rows_out[to, slot * BB : (slot + 1) * BB, :] = resid[block_in(to, slot)]
 
         @pl.when(k < peers)
         def _():
@@ -356,32 +407,10 @@
     sample_rows, columns = visibilities.shape
     comps = comp_lm.shape[1]
     block_count = sample_rows // BB
-    group_rows = sample_rows // owners
     slots = max(2, 2 * block_count // peers)
     share = PIX // owners
 
-    directions = jnp.arange(DIR_DEV, dtype=jnp.int32)
-    place = jnp.sum(
-        jnp.where(peel_order[:, None] == directions[None, :], directions[:, None], 0), axis=0
-    )
-    place = jnp.broadcast_to(place[:, None], (DIR_DEV, comps // DIR_DEV)).reshape(comps)
-    entries = jnp.stack([assignment, place])
-
-    tile_ids = block_tile[:, 0]
-    block_ids = jnp.arange(block_count, dtype=jnp.int32)
-    same_tile = tile_ids[:, None] == tile_ids[None, :]
-    before = block_ids[None, :] < block_ids[:, None]
-    slot_index = jnp.sum(same_tile & before, axis=1, dtype=jnp.int32)
-    target = tile_ids * slots + slot_index
-    placed = target[None, :] == jnp.arange(peers * slots, dtype=jnp.int32)[:, None]
-    block_of = jnp.min(jnp.where(placed, block_ids[None, :], block_count), axis=1)
-    block_coords = uv_coords.reshape(2, block_count, BB).transpose(1, 0, 2).reshape(block_count, -1)
-    send_coords = jnp.dot(placed.astype(BF16), block_coords, preferred_element_type=F32)
-    send_coords = send_coords.astype(BF16).reshape(peers, slots, 2, BB).transpose(0, 2, 1, 3)
-    send_coords = jnp.pad(
-        send_coords.reshape(peers, 2, slots * BB), ((0, 0), (0, 14), (0, 0))
-    )
-
+    slot_lanes = -(-peers * slots // LANES) * LANES
     vmem = pl.BlockSpec(memory_space=pltpu.VMEM)
     smem = pl.BlockSpec(memory_space=pltpu.SMEM)
     dma = pltpu.SemaphoreType.DMA
@@ -391,19 +420,24 @@
             jax.ShapeDtypeStruct((sample_rows, columns), BF16),
             jax.ShapeDtypeStruct((2, share, columns), F32),
         ),
-        in_specs=[vmem] * 6 + [smem, vmem],
+        in_specs=[vmem] * 7 + [smem],
         out_specs=(vmem, vmem),
         scratch_shapes=[
             pltpu.VMEM((2, comps, DIR_DEV * columns), BF16),
-            pltpu.VMEM((2, group_rows, CHUNK), BF16),
-            pltpu.VMEM((2, group_rows, CHUNK), BF16),
-            pltpu.VMEM((group_rows, DIR_DEV * columns), F32),
-            pltpu.VMEM((owners, group_rows, DIR_DEV * columns), BF16),
-            pltpu.VMEM((owners, group_rows, DIR_DEV * columns), BF16),
+            pltpu.VMEM((8, comps), BF16),
+            pltpu.VMEM((block_count + 1, BB, LANES), BF16),
+            pltpu.VMEM((1, slot_lanes), jnp.int32),
+            pltpu.SMEM((1, slot_lanes), jnp.int32),
+            pltpu.VMEM((peers, slots * BB, LANES), BF16),
+            pltpu.VMEM((2, sample_rows // owners, CHUNK), BF16),
+            pltpu.VMEM((2, sample_rows // owners, CHUNK), BF16),
+            pltpu.VMEM((sample_rows // owners, DIR_DEV * columns), F32),
+            pltpu.VMEM((owners, sample_rows // owners, DIR_DEV * columns), BF16),
+            pltpu.VMEM((owners, sample_rows // owners, DIR_DEV * columns), BF16),
             pltpu.VMEM((block_count + 1, BB, columns), BF16),
             pltpu.VMEM((peers, slots * BB, columns), BF16),
             pltpu.VMEM((peers, slots * BB, columns), BF16),
-            pltpu.VMEM((peers, 16, slots * BB), BF16),
+            pltpu.VMEM((peers, slots * BB, LANES), BF16),
             pltpu.VMEM((peers, 2 * share, slots * BB), BF16),
             dma((owners,)),
             dma((owners,)),
@@ -413,19 +447,20 @@
             dma((peers,)),
             dma((peers,)),
             dma((peers,)),
+            dma,
         ],
         compiler_params=pltpu.CompilerParams(
             collective_id=0, has_side_effects=True, vmem_limit_bytes=60 * 1024 * 1024
         ),
     )(
         visibilities,
-        uv_coords.astype(F32).T,
+        uv_coords,
         comp_lm,
         spectra,
         ridge_weight[None, :],
-        entries,
-        block_of,
-        send_coords,
+        assignment.reshape(comps // LANES, LANES),
+        block_tile,
+        peel_order,
     )
     return residual, subgrid[None]
 

time: 59.3 us -> 54.5 us (0.919)
  other arithmetic: 4.33 us -> 0 us
  Pallas kernels: 46.9 us -> 49 us
  local copies, waits for them, and re-layouts: 6.78 us -> 4.68 us
    pallas_call x1, Pallas kernels: 46.9 us -> 49 us  [local(): pl.pallas_call(functools.partial(kernel, owners, peers, slots), out_shape...]
    transpose x1 -> x0, local copies, waits for them, and re-layouts: 1.65 us -> none  [local(): uv_coords.astype(F32)]
    reduce_sum x2 -> x0, other arithmetic: 1.65 us -> none  [the longest x1 0.91 us: local(): slot_index = jnp.sum(same_tile & before, axis=1, dtype=jnp.int32)]
    another operation x1 -> x0, other arithmetic: 1.34 us -> none  [local(): entries = jnp.stack([assignment, place])]
    unnamed x4 -> x3, local copies, waits for them, and re-layouts: 3.42 us -> 4.68 us
    reshape x6 -> x0, local copies, waits for them, and re-layouts: 1.06 us -> none  [the longest x3 0.87 us: local(): uv_coords.reshape(2, block_count, BB).transpose(1, 0, 2)]
    reduce_min x1 -> x0, other arithmetic: 0.68 us -> none  [local(): jnp.min(jnp.where(placed, block_ids[None, :], block_count), axis=1)]
    add x1 -> x0, other arithmetic: 0.66 us -> none  [local(): target = tile_ids * slots + slot_index]
where the time goes in v1:
time: 54.5 us; the launch traced here: 54.3 us
  Pallas kernels  49 us (90%)
  local copies, waits for them, and re-layouts  4.68 us (9%)
  between operations  0.64 us (1%)
    pallas_call x1, Pallas kernels, local(): pl.pallas_call(functools.partial(kernel, owners, peers, slots), out_shape...  49 us
    unnamed x3, local copies, waits for them, and re-layouts  4.68 us

profile of v1, /device:TPU:13, one launch (start us, length us, event | category | flops | bytes accessed | tf_op | source)
XLA Modules:
  0.0 54.3 jit_solution(13508123258294111630)
XLA Ops:
  0.6 1.3 %copy.10.tile_ref = s32[32,1]{1,0:T(8,128)} copy(s32[32,1]{0,1:T(1,128)} %param.15) | data formatting | bytes 256 | tf_op args[7]
  2.0 49.0 %shard_map.95 = (bf16[1024,128]{1,0:T(8,128)(2,1)}, f32[2,256,128]{2,1,0:T(8,128)}) custom-call(bf16[1024,128]{1,0:T(8,128)(2,1)} %vis_ref.1, bf16[2,1024]{1,0:T(2,128)(2,1)} %uv_ref.1, f32[2,3072]{1,0:T(2,128)} %lm_ref.1, bf16[2,3072,128]{2,1,0:T(8,128)(2,1)} %spec_ref.1, f32[1,128]{1,0:T(1,128)} %bitcast.5, s32[24,128]{1,0:T(8,128)} %bitcast.4, ...), custom_call_target="tpu_custom_call" | custom-call | tf_op jit(solution)/shard_map/pallas_call | solution.py:417
  51.0 1.7 %copy.13 = bf16[1024,128]{1,0:T(8,128)(2,1)} copy(bf16[1024,128]{1,0:T(8,128)(2,1)} %get-tuple-element.8) | data formatting | bytes 524288
  52.6 1.7 %copy.14 = f32[1,2,256,128]{3,2,1,0:T(8,128)} copy(f32[1,2,256,128]{3,2,1,0:T(8,128)} %bitcast.3) | data formatting | bytes 524288

commit v2 on v1

--- a/solution.py
+++ b/solution.py
@@ -108,19 +108,29 @@
     pl.semaphore_wait(barrier, owners - 1 + peers - 1)
 
     slot_lanes = block_row.shape[1]
-    lane = lax.broadcasted_iota(jnp.int32, (block_count, slot_lanes), 1)
-    tile = jnp.broadcast_to(tile_ref[...], (block_count, slot_lanes))
-    named_tile = jnp.where(lane == tile, 1.0, 0.0)
-    row_id = lax.broadcasted_iota(jnp.int32, (block_count, block_count), 0)
+    tiles = jnp.broadcast_to(tile_ref[...], (slot_lanes, block_count))
+    named_tile = jnp.where(
+        lax.broadcasted_iota(jnp.int32, (slot_lanes, block_count), 0) == tiles, 1.0, 0.0
+    )
     earlier = jnp.where(
-        lax.broadcasted_iota(jnp.int32, (block_count, block_count), 1) < row_id, 1.0, 0.0
-    )
-    ranks = jnp.dot(earlier.astype(BF16), named_tile.astype(BF16), preferred_element_type=F32)
-    slot = jnp.sum(ranks * named_tile, axis=1, keepdims=True).astype(jnp.int32)
-    target = tile_ref[...] * slots + slot
-    block_id = lax.broadcasted_iota(jnp.int32, (block_count, slot_lanes), 0)
-    taken = jnp.where(lane == target, block_id, block_count).astype(F32)
-    block_row[...] = jnp.min(taken, axis=0, keepdims=True).astype(jnp.int32)
+        lax.broadcasted_iota(jnp.int32, (block_count, block_count), 0)
+        < lax.broadcasted_iota(jnp.int32, (block_count, block_count), 1),
+        1.0,
+        0.0,
+    )
+    ranks = jnp.dot(named_tile.astype(BF16), earlier.astype(BF16), preferred_element_type=F32)
+    slot = jnp.sum(ranks * named_tile, axis=0, keepdims=True).astype(jnp.int32)
+    target = jnp.broadcast_to(tile_ref[...] * slots + slot, (slot_lanes, block_count))
+    lane = lax.broadcasted_iota(jnp.int32, (slot_lanes, block_count), 0)
+    taken = jnp.where(lane == target, 1.0, 0.0).astype(BF16)
+    block_id = lax.broadcasted_iota(jnp.int32, (8, block_count), 1) - block_count
+    picked = lax.dot_general(
+        block_id.astype(F32).astype(BF16),
+        taken,
+        (((1,), (1,)), ((), ())),
+        preferred_element_type=F32,
+    )
+    block_row[...] = picked[0:1, :].astype(jnp.int32) + block_count
     index_copy = pltpu.make_async_copy(block_row, block_of_ref, index_sem)
     index_copy.start()
 
@@ -215,24 +225,46 @@
         group = lax.rem(me_d + k, owners)
         group_coords = coord_rows[pl.ds(group * group_blocks, group_blocks)]
         group_coords = group_coords.reshape(group_rows, LANES)[:, 0:8]
-        for chunk in range(comps // CHUNK):
-            turned = turned_a if chunk % 2 == 0 else turned_b
-            span = slice(chunk * CHUNK, (chunk + 1) * CHUNK)
-            turns = jnp.dot(group_coords, lm_parts[:, span], preferred_element_type=F32)
-            for sub in range(group_rows // SUB):
+        chunks = comps // CHUNK
+        buffers = (turned_a, turned_b)
+        pieces = group_rows // SUB
+
+        def spread_turns(chunk):
+            return jnp.dot(
+                group_coords,
+                lm_parts[:, chunk * CHUNK : (chunk + 1) * CHUNK],
+                preferred_element_type=F32,
+            )
+
+        def contract_chunk(chunk, part):
+            return jnp.dot(
+                buffers[chunk % 2][part],
+                masked[part, chunk * CHUNK : (chunk + 1) * CHUNK, :],
+                preferred_element_type=F32,
+            )
+
+        turns = spread_turns(0)
+        for chunk in range(chunks):
+            turned = buffers[chunk % 2]
+            following = None
+            for sub in range(pieces):
                 rows = slice(sub * SUB, (sub + 1) * SUB)
                 cos_part, sin_part = turn_cos_sin(turns[rows])
                 turned[0, rows, :] = cos_part
                 turned[1, rows, :] = sin_part
-            update = jnp.dot(turned[0], masked[0, span, :], preferred_element_type=F32) + jnp.dot(
-                turned[1], masked[1, span, :], preferred_element_type=F32
-            )
-            if chunk == 0:
-                acc[...] = update
-            elif chunk < comps // CHUNK - 1:
-                acc[...] += update
-            else:
-                final = (acc[...] + update).astype(BF16)
+                if chunk > 0 and sub == 0:
+                    update = contract_chunk(chunk - 1, 0)
+                if chunk > 0 and sub == pieces // 2 - 1:
+                    update = update + contract_chunk(chunk - 1, 1)
+                    if chunk == 1:
+                        acc[...] = update
+                    else:
+                        acc[...] += update
+                if chunk + 1 < chunks and sub == pieces - 2:
+                    following = spread_turns(chunk + 1)
+            turns = following
+        last = contract_chunk(chunks - 1, 0) + contract_chunk(chunks - 1, 1)
+        final = (acc[...] + last).astype(BF16)
 
         @pl.when(k < owners)
         def _():
@@ -459,7 +491,7 @@
         spectra,
         ridge_weight[None, :],
         assignment.reshape(comps // LANES, LANES),
-        block_tile,
+        block_tile.reshape(1, block_count),
         peel_order,
     )
     return residual, subgrid[None]

time: 54.5 us -> 51.3 us (0.941)
  Pallas kernels: 49 us -> 47.1 us
  local copies, waits for them, and re-layouts: 4.68 us -> 3.34 us
    pallas_call x1, Pallas kernels: 49 us -> 47.1 us  [local(): pl.pallas_call(functools.partial(kernel, owners, peers, slots), out_shape...]
    unnamed x3 -> x2, local copies, waits for them, and re-layouts: 4.68 us -> 3.34 us
where the time goes in v2:
time: 51.3 us; the launch traced here: 51.1 us
  Pallas kernels  47.1 us (92%)
  local copies, waits for them, and re-layouts  3.34 us (7%)
  between operations  0.64 us (1%)
    pallas_call x1, Pallas kernels, local(): pl.pallas_call(functools.partial(kernel, owners, peers, slots), out_shape...  47.1 us
    unnamed x2, local copies, waits for them, and re-layouts  3.34 us

profile of v2, /device:TPU:13, one launch (start us, length us, event | category | flops | bytes accessed | tf_op | source)
XLA Modules:
  0.0 51.1 jit_solution(8292949478352147592)
XLA Ops:
  0.6 47.1 %shard_map.95 = (bf16[1024,128]{1,0:T(8,128)(2,1)}, f32[2,256,128]{2,1,0:T(8,128)}) custom-call(bf16[1024,128]{1,0:T(8,128)(2,1)} %vis_ref.1, bf16[2,1024]{1,0:T(2,128)(2,1)} %uv_ref.1, f32[2,3072]{1,0:T(2,128)} %lm_ref.1, bf16[2,3072,128]{2,1,0:T(8,128)(2,1)} %spec_ref.1, f32[1,128]{1,0:T(1,128)} %bitcast.6, s32[24,128]{1,0:T(8,128)} %bitcast.5, ...), custom_call_target="tpu_custom_call" | custom-call | tf_op jit(solution)/shard_map/pallas_call | solution.py:449
  47.7 1.7 %copy.12 = bf16[1024,128]{1,0:T(8,128)(2,1)} copy(bf16[1024,128]{1,0:T(8,128)(2,1)} %get-tuple-element.8) | data formatting | bytes 524288
  49.4 1.7 %copy.13 = f32[1,2,256,128]{3,2,1,0:T(8,128)} copy(f32[1,2,256,128]{3,2,1,0:T(8,128)} %bitcast.4) | data formatting | bytes 524288

commit v3 on v2

--- a/solution.py
+++ b/solution.py
@@ -21,7 +21,7 @@
 F32 = jnp.float32
 BF16 = jnp.bfloat16
 LANES = 128
-CHUNK = 512
+CHUNK = 256
 SUB = 32
 
 SIN_FIT = (4.4428795675460835, -7.307816684491791, 3.5977741780872416, -0.7911993921613704)
@@ -172,14 +172,14 @@
         at_low, at_high, (((1,), (1,)), ((), ())), preferred_element_type=F32
     )
     for strip in range(strips):
-        own = jnp.broadcast_to(positions[:, strip : strip + 1], (LANES, columns))
+        own = jnp.broadcast_to(positions[:, strip : strip + 1], (LANES, columns)).astype(BF16)
         span = pl.ds(strip * LANES, LANES)
         for part in range(2):
-            values = spec_ref[part, span, :].astype(F32)
+            values = spec_ref[part, span, :]
             for position in range(DIR_DEV):
                 masked[part, span, position * columns : (position + 1) * columns] = jnp.where(
-                    own == float(position), values, 0.0
-                ).astype(BF16)
+                    own == jnp.asarray(position, BF16), values, jnp.zeros_like(values)
+                )
 
     def coords_copy(src, owner, to):
         return pltpu.make_async_remote_copy(
@@ -422,6 +422,17 @@
         return carry
 
     lax.fori_loop(1, peers, drain, 0)
+
+
+def finish(resid_ref, grid_ref, resid_out, grid_out, sem):
+    copies = (
+        pltpu.make_async_copy(resid_ref, resid_out, sem.at[0]),
+        pltpu.make_async_copy(grid_ref, grid_out, sem.at[1]),
+    )
+    for copy in copies:
+        copy.start()
+    for copy in copies:
+        copy.wait()
 
 
 def local(
@@ -494,6 +505,17 @@
         block_tile.reshape(1, block_count),
         peel_order,
     )
+    anywhere = pl.BlockSpec(memory_space=pl.ANY)
+    residual, subgrid = pl.pallas_call(
+        finish,
+        out_shape=(
+            jax.ShapeDtypeStruct(residual.shape, residual.dtype),
+            jax.ShapeDtypeStruct(subgrid.shape, subgrid.dtype),
+        ),
+        in_specs=[vmem] * 2,
+        out_specs=(anywhere, anywhere),
+        scratch_shapes=[dma((2,))],
+    )(residual, subgrid)
     return residual, subgrid[None]
 
 

time: 51.3 us -> 49.2 us (0.959)
  local copies, waits for them, and re-layouts: 3.34 us -> 0 us
  Pallas kernels: 47.1 us -> 48.4 us
    unnamed x2 -> x0, local copies, waits for them, and re-layouts: 3.34 us -> none
    pallas_call x0 -> x1, Pallas kernels: none -> 1.83 us  [local(): pl.pallas_call(finish, out_shape=(jax.ShapeDtypeStruct(residual.shape, re...]
    pallas_call x1, Pallas kernels: 47.1 us -> 46.5 us  [local(): pl.pallas_call(functools.partial(kernel, owners, peers, slots), out_shape...]
where the time goes in v3:
time: 49.2 us; the launch traced here: 49 us
  Pallas kernels  48.4 us (98%)
  between operations  0.64 us (1%)
    pallas_call x1, Pallas kernels, local(): pl.pallas_call(functools.partial(kernel, owners, peers, slots), out_shape...  46.5 us
    pallas_call x1, Pallas kernels, local(): pl.pallas_call(finish, out_shape=(jax.ShapeDtypeStruct(residual.shape, re...  1.83 us

profile of v3, /device:TPU:13, one launch (start us, length us, event | category | flops | bytes accessed | tf_op | source)
XLA Modules:
  0.0 49.0 jit_solution(2786233981317991042)
XLA Ops:
  0.6 46.5 %shard_map.95 = (bf16[1024,128]{1,0:T(8,128)(2,1)}, f32[2,256,128]{2,1,0:T(8,128)}) custom-call(bf16[1024,128]{1,0:T(8,128)(2,1)} %vis_ref.1, bf16[2,1024]{1,0:T(2,128)(2,1)} %uv_ref.1, f32[2,3072]{1,0:T(2,128)} %lm_ref.1, bf16[2,3072,128]{2,1,0:T(8,128)(2,1)} %spec_ref.1, f32[1,128]{1,0:T(1,128)} %bitcast.5, s32[24,128]{1,0:T(8,128)} %bitcast.4, ...), custom_call_target="tpu_custom_call" | custom-call | tf_op jit(solution)/shard_map/pallas_call | solution.py:460
  47.2 1.8 %shard_map.96 = (bf16[1024,128]{1,0:T(8,128)(2,1)}, f32[2,256,128]{2,1,0:T(8,128)}) custom-call(bf16[1024,128]{1,0:T(8,128)(2,1)} %get-tuple-element.6.resid_ref, f32[2,256,128]{2,1,0:T(8,128)} %get-tuple-element.7.grid_ref), custom_call_target="tpu_custom_call" | custom-call | tf_op jit(solution)/shard_map/pallas_call | solution.py:509
